TPU v7x, 512 devices: a whole 4x4x16 slice. The times are simulated.
512 devices in a mesh: ctx: 64 (over y, z), exp: 8 (over x, core).
Axes of the slice: x: 4, y: 4, z: 16, core: 2. Of those that a mesh axis runs over, the one named last changes fastest.
Arguments:
- queries: bfloat16 [8192, 4096], P('ctx', 'exp'), may hold values from -24 to 24
- key_rows: bfloat16 [8192, 1024], P('ctx', 'exp'), may hold values from -24 to 24
- mixer_input: bfloat16 [8192, 8192], P('ctx', 'exp'), may hold values from -32 to 32
- gate_input: bfloat16 [8192, 8192], P('ctx', 'exp'), may hold values from -6 to 6
- write_proj: bfloat16 [8192, 128], P('ctx'), may hold values from -0.5 to 0.5
- read_proj: bfloat16 [8192, 128], P('ctx'), may hold values from -0.5 to 0.5
- step_size: float32 [8192, 128], P('ctx', 'exp'), may hold values from 0.5 to 2
- log_decay: float32 [8192, 128], P('ctx', 'exp'), may hold values from -1.7 to 0
- skip_gain: float32 [128], P('exp'), may hold values from 0.5 to 2
- norm_gain: float32 [8192], P('exp'), may hold values from 0.1 to 1.9
- value_weight: bfloat16 [8192, 1024], P('exp'), may hold values from -0.09375 to 0.09375
Outputs:
- attention_out: bfloat16 [8192, 4096], P('ctx', 'exp')
- mixer_out: bfloat16 [8192, 8192], P('ctx', 'exp')
All inputs are finite; a program needn't handle non-finite values.
Results may differ from a plain program's by a relative error of at most 0.018.
Values may be sent and summed in bfloat16 or wider, within the bound.
A program may use at most 64 MiB of HBM per device.

v0:
```python
import jax
import jax.numpy as jnp
from jax import lax
from jax.sharding import PartitionSpec as P

QUERY_HEADS = 32
KEY_HEADS = 8
HEAD_DIM = 128
MIXER_HEADS = 128
MIXER_CHANNELS = 64
STATE_SIZE = 128
BLOCK_LEN = 128
rope_base = 10000.0
rope_stretch = 4.0
norm_eps = 1e-05
floor_score = -1e30


def entering(x, axis, join, neutral):
    place = lax.axis_index(axis)
    gathered = jax.tree.map(
        lambda a, kind: lax.all_gather(a.astype(kind), axis), x, (jnp.bfloat16, jnp.bfloat16)
    )
    state = jax.tree.map(lambda a, e: jnp.zeros_like(a) + jnp.asarray(e, a.dtype), x, neutral)

    def one(lap, state):
        return join(
            state,
            jax.tree.map(
                lambda a, own: lax.dynamic_index_in_dim(a, lap, 0, False).astype(own.dtype),
                gathered,
                x,
            ),
        )

    return lax.fori_loop(0, place, one, state)


def rotate(vectors, positions, head_width):
    halfway = head_width // 2
    frequency = rope_base ** (-(2.0 * jnp.arange(halfway, dtype=jnp.float32)) / head_width)
    angles = (positions.astype(jnp.float32) / rope_stretch)[:, None] * frequency[None, :]
    cosine = jnp.cos(angles)[:, None, :]
    sine_part = jnp.sin(angles)[:, None, :]
    front_half = vectors[..., :halfway].astype(jnp.float32)
    back_half = vectors[..., halfway:].astype(jnp.float32)
    turned = jnp.concatenate(
        [front_half * cosine - back_half * sine_part, back_half * cosine + front_half * sine_part],
        axis=-1,
    )
    return turned.astype(jnp.bfloat16)


def attend_update(
    running, query_group, query_pos, key_block, value_block, key_pos, group_low, group_high
):
    running_max, running_sum, running_out = running
    scores = jnp.einsum(
        "cgtd,scd->cgts", query_group, key_block, preferred_element_type=jnp.float32
    ) * HEAD_DIM ** (-0.5)
    allowed = key_pos[None, :] <= query_pos[:, None]
    masked = jnp.where(allowed, scores, floor_score)
    new_max = jnp.maximum(running_max, jnp.max(masked, axis=-1))
    weights = jnp.where(allowed, jnp.exp(masked - new_max[..., None]), 0.0)
    factor = jnp.exp(running_max - new_max)
    new_sum = running_sum * factor + jnp.sum(weights, axis=-1)
    update = jnp.einsum(
        "cgts,scd->cgtd",
        weights.astype(jnp.bfloat16),
        value_block,
        preferred_element_type=jnp.float32,
    )
    new_out = running_out * factor[..., None] + update
    return (
        running_max.at[:, :, group_low:group_high].set(new_max),
        running_sum.at[:, :, group_low:group_high].set(new_sum),
        running_out.at[:, :, group_low:group_high].set(new_out),
    )


def attention(queries, key_rows, value_rows):
    row_count = queries.shape[0]
    kv_local = key_rows.shape[1] // HEAD_DIM
    group_size = QUERY_HEADS // KEY_HEADS
    shard_index = lax.axis_index("ctx")
    local_pos = jnp.arange(row_count, dtype=jnp.int32)
    groups = ((0, row_count),)
    query_pos = shard_index * row_count + local_pos
    turned_q = rotate(
        queries.reshape(row_count, kv_local * group_size, HEAD_DIM), query_pos, HEAD_DIM
    )
    query_mat = jnp.transpose(
        turned_q.reshape(row_count, kv_local, group_size, HEAD_DIM), (1, 2, 0, 3)
    )
    turned_k = rotate(key_rows.reshape(row_count, kv_local, HEAD_DIM), query_pos, HEAD_DIM)
    value_mat = value_rows.reshape(row_count, kv_local, HEAD_DIM)
    initial = (
        jnp.full((kv_local, group_size, row_count), floor_score, jnp.float32),
        jnp.zeros((kv_local, group_size, row_count), jnp.float32),
        jnp.zeros((kv_local, group_size, row_count, HEAD_DIM), jnp.float32),
    )
    piece_keys = lax.all_gather(turned_k, "ctx", axis=0, tiled=True)
    piece_values = lax.all_gather(value_mat, "ctx", axis=0, tiled=True)
    piece_rows = piece_keys.shape[0]
    piece_pos = jnp.arange(piece_rows, dtype=jnp.int32)

    def key_step(step_index, current):
        offset = step_index * row_count
        block_keys = lax.dynamic_slice_in_dim(piece_keys, offset, row_count, 0)
        block_values = lax.dynamic_slice_in_dim(piece_values, offset, row_count, 0)
        block_pos = lax.dynamic_slice_in_dim(piece_pos, offset, row_count, 0)
        group_low, group_high = groups[0]
        group_pos = query_pos

        def group_update(state_in, group_low=group_low, group_high=group_high, group_pos=group_pos):
            return attend_update(
                state_in,
                query_mat,
                group_pos,
                block_keys,
                block_values,
                block_pos,
                group_low,
                group_high,
            )

        def unchanged(state_in):
            return state_in

        needed = jnp.min(block_pos) <= jnp.max(group_pos)
        current = lax.cond(needed, group_update, unchanged, current)
        return current

    result = lax.fori_loop(0, piece_rows // row_count, key_step, initial)
    running_max, running_sum, running_out = result
    merged = running_out / running_sum[..., None]
    finished = (
        jnp.transpose(merged, (2, 0, 1, 3))
        .reshape(row_count, kv_local * group_size * HEAD_DIM)
        .astype(jnp.bfloat16)
    )
    return finished


def chain_join(earlier, later):
    return (earlier[0] + later[0], jnp.exp(later[0])[:, None, None] * earlier[1] + later[1])


def mixer_block(
    mixer_input, gate_input, write_proj, read_proj, step_size, log_decay, skip_gain, norm_gain
):
    row_count = mixer_input.shape[0]
    head_count = step_size.shape[1]
    block_count = row_count // BLOCK_LEN
    shaped_x = mixer_input.reshape(block_count, BLOCK_LEN, head_count, MIXER_CHANNELS)
    causal = jnp.arange(BLOCK_LEN)[:, None] >= jnp.arange(BLOCK_LEN)[None, :]
    agg_state = jnp.zeros((head_count, MIXER_CHANNELS, STATE_SIZE), jnp.float32)
    block_x = shaped_x[0]
    block_read = read_proj
    cumul = jnp.cumsum(log_decay, axis=0)
    gram = jnp.einsum("tn,sn->ts", block_read, write_proj, preferred_element_type=jnp.float32)
    cumul_heads = cumul.T
    spread = cumul_heads[:, :, None] - cumul_heads[:, None, :]
    decay = jnp.where(causal[None], jnp.exp(jnp.where(causal[None], spread, 0.0)), 0.0)
    mixing = (decay * gram[None] * step_size.T[:, None, :]).astype(jnp.bfloat16)
    intra = jnp.einsum("hts,shp->thp", mixing, block_x, preferred_element_type=jnp.float32)
    ending = cumul[-1]
    weighted = (
        block_x.astype(jnp.float32) * (step_size * jnp.exp(ending[None, :] - cumul))[:, :, None]
    ).astype(jnp.bfloat16)
    local_state = jnp.einsum(
        "shp,sn->hpn", weighted, write_proj, preferred_element_type=jnp.float32
    )
    agg_state = jnp.exp(ending)[:, None, None] * agg_state + local_state
    agg_decay = ending
    saved = (intra, cumul, ending, local_state, block_read, block_x)
    incoming = entering(
        (agg_decay, agg_state),
        "ctx",
        chain_join,
        (
            jnp.zeros((head_count,), jnp.float32),
            jnp.zeros((head_count, MIXER_CHANNELS, STATE_SIZE), jnp.float32),
        ),
    )
    carried = incoming[1]
    intra, cumul, ending, local_state, block_read, block_x = saved
    inter = (
        jnp.einsum(
            "tn,hpn->thp", block_read.astype(jnp.float32), carried, precision=lax.Precision.HIGHEST
        )
        * jnp.exp(cumul)[:, :, None]
    )
    pieces_out = intra + inter + skip_gain[None, :, None] * block_x.astype(jnp.float32)
    gate_full = gate_input.reshape(row_count, head_count, MIXER_CHANNELS).astype(jnp.float32)
    gated = pieces_out * jax.nn.silu(gate_full)
    partial_square = jnp.sum(gated * gated, axis=(1, 2))
    total_square = lax.psum(partial_square, "exp")
    mean_square = total_square / (MIXER_HEADS * MIXER_CHANNELS)
    normed = (
        gated
        * lax.rsqrt(mean_square + norm_eps)[:, None, None]
        * norm_gain.reshape(head_count, MIXER_CHANNELS)
    )
    return normed.reshape(row_count, head_count * MIXER_CHANNELS).astype(jnp.bfloat16)


def on_device(
    queries,
    key_rows,
    mixer_input,
    gate_input,
    write_proj,
    read_proj,
    step_size,
    log_decay,
    skip_gain,
    norm_gain,
    value_weight,
):
    mixer_out = mixer_block(
        mixer_input, gate_input, write_proj, read_proj, step_size, log_decay, skip_gain, norm_gain
    )
    value_terms = jnp.dot(mixer_out, value_weight, preferred_element_type=jnp.float32)
    value_rows = lax.psum_scatter(
        value_terms.astype(jnp.bfloat16), "exp", scatter_dimension=1, tiled=True
    )
    attention_out = attention(queries, key_rows, value_rows)
    return (attention_out, mixer_out)


def solution(mesh):
    return jax.shard_map(
        on_device,
        mesh=mesh,
        in_specs=(
            P("ctx", "exp"),
            P("ctx", "exp"),
            P("ctx", "exp"),
            P("ctx", "exp"),
            P("ctx", None),
            P("ctx", None),
            P("ctx", "exp"),
            P("ctx", "exp"),
            P("exp"),
            P("exp"),
            P("exp", None),
        ),
        out_specs=(P("ctx", "exp"), P("ctx", "exp")),
        check_vma=False,
    )
```

profile of v0, /device:TPU:504, one launch (start us, length us, event | category | flops | bytes accessed | tf_op | source)
XLA Modules:
  0.0 883.1 jit_solution(17325050694433945698)
XLA Ops:
  12.2 70.4 %all-gather.2 = bf16[64,1,16]{2,1,0:T(2,128)(2,1)S(1)} all-gather(bf16[1,1,16]{2,1,0:T(2,128)(2,1)S(1)} %convert_bitcast_fusion), channel_id=1, replica_groups=mesh['ctx'=64,'exp'=8] {'ctx'}, dimensions={0}, use_global_device_ids=true | all-gather | bytes 2080 | tf_op jit(solution)/shard_map/all_gather | solution.py:22
  84.7 114.7 %all-gather.9.cloned.1.call-done = bf16[1024,64,128]{2,1,0:T(8,128)(2,1)} async-done(((bf16[16,64,128]{2,1,0:T(8,128)(2,1)}), bf16[1024,64,128]{2,1,0:T(8,128)(2,1)}) %all-gather.9.cloned.1.call-update) | async-done | bytes 16777232 | tf_op jit(solution)/shard_map/all_gather | solution.py:22
  199.5 73.2 %while.37 = (s32[]{:T(128)}, f32[16,64,128]{2,1,0:T(8,128)S(1)}, s32[]{:T(128)}, bf16[64,16]{1,0:T(8,128)(2,1)S(1)}, bf16[64,16,64,128]{3,2,1,0:T(8,128)(2,1)}, /*index=5*/s32[]{:T(128)}, s32[]{:T(128)}, s32[]{:T(128)}) while((s32[]{:T(128)}, f32[16,64,128]{2,1,0:T(8,128)S(1)}, s32[]{:T(128)}, bf16[64,16]{1,0:T(8,128)(2,1)S(1)}, ...), condition=%wide.region_2.3_spmd, body=%wide.region_1.2_spmd.sunk | while | flops 393237 | bytes 1311007 | solution.py:36
  272.6 2.3 multiply_reduce_fusion
  275.0 13.8 %psum.7 = f32[128]{0:T(128)S(1)} all-reduce(f32[128]{0:T(128)S(1)} %get-tuple-element.521), channel_id=1, replica_groups=mesh['ctx'=64,'exp'=8] {'exp'}, use_global_device_ids=true, to_apply=%region_4.5 | all-reduce | flops 128 | bytes 1024 | tf_op jit(solution)/shard_map/psum | solution.py:198
  292.4 29.7 %reduce-scatter.4.cloned.1.call-done = bf16[128,128]{1,0:T(8,128)(2,1)} async-done(((bf16[1024,128]{1,0:T(8,128)(2,1)}), bf16[128,128]{1,0:T(8,128)(2,1)}) %reduce-scatter.4.cloned.1.call-update) | async-done | bytes 32784
  324.8 132.9 %all-gather.7.cloned.1.call-done = bf16[8192,1,128]{0,2,1:T(8,128)(2,1)} async-done(((bf16[128,1,128]{0,2,1:T(8,128)(2,1)}), bf16[8192,1,128]{0,2,1:T(8,128)(2,1)}) %all-gather.7.cloned.1.call-update) | async-done | bytes 2097168 | tf_op jit(solution)/shard_map/all_gather | solution.py:102
  457.7 4.1 copy.67
  462.6 134.0 %all-gather.11.cloned.1.call-done = bf16[8192,128]{1,0:T(8,128)(2,1)} async-done(((bf16[128,128]{1,0:T(8,128)(2,1)}), bf16[8192,128]{1,0:T(8,128)(2,1)}) %all-gather.11.cloned.1.call-update) | async-done | bytes 2097168 | tf_op jit(solution)/shard_map/all_gather | solution.py:103
  596.7 278.9 %while.38 = (s32[]{:T(128)}, f32[1,4,128]{2,1,0:T(4,128)S(1)}, f32[1,4,128]{2,1,0:T(4,128)S(1)}, f32[1,4,128,128]{3,2,1,0:T(8,128)S(1)}, s32[8192]{0:T(1024)S(1)...) while((s32[]{:T(128)}, f32[1,4,128]{2,1,0:T(4,128)S(1)}, ...), condition=%wide.region_13.14_spmd.clone, body=%wide.region_7.0_spmd.clone.sunk | while | flops 34293512 | bytes 1610581 | solution.py:134
  598.8 2.2 conditional.3
  603.2 2.2 conditional.3
  607.5 2.2 conditional.3
  611.9 2.2 conditional.3
  620.6 2.2 conditional.3
  624.9 2.2 conditional.3
  629.3 2.2 conditional.3
  638.0 2.2 conditional.3
  642.4 2.2 conditional.3
  646.7 2.2 conditional.3
  655.4 2.2 conditional.3
  659.8 2.2 conditional.3
  664.2 2.2 conditional.3
  672.9 2.2 conditional.3
  677.2 2.2 conditional.3
  681.6 2.2 conditional.3
  690.3 2.2 conditional.3
  699.0 2.2 conditional.3
  707.7 2.2 conditional.3
  716.5 2.2 conditional.3
  725.2 2.2 conditional.3
  733.9 2.2 conditional.3
  742.6 2.2 conditional.3
  751.3 2.2 conditional.3
  760.0 2.2 conditional.3
  768.8 2.2 conditional.3
  777.5 2.2 conditional.3
  786.2 2.2 conditional.3
  794.9 2.2 conditional.3
  803.6 2.2 conditional.3
  812.3 2.2 conditional.3
  821.0 2.2 conditional.3
  829.8 2.2 conditional.3
  838.5 2.2 conditional.3
  847.2 2.2 conditional.3
  855.9 2.2 conditional.3
  864.6 2.2 conditional.3
  873.3 2.2 conditional.3
  (861 shorter events, 333.5 us)
Async XLA Ops:
  7.2 282.9 %copy-start = (bf16[1024,1024]{1,0:T(8,128)(2,1)S(1)}, bf16[1024,1024]{1,0:T(8,128)(2,1)}, u32[]{:S(2)}) copy-start(bf16[1024,1024]{1,0:T(8,128)(2,1)} %param.39) | copy-start | bytes 6291460
  7.2 76.1 %copy-start.6 = (f32[128,16]{0,1:T(8,128)S(1)}, f32[128,16]{0,1:T(8,128)}, u32[]{:S(2)}) copy-start(f32[128,16]{0,1:T(8,128)} %param.35) | copy-start | bytes 24580
  7.2 76.0 %copy-start.3 = (bf16[128,128]{1,0:T(8,128)(2,1)S(1)}, bf16[128,128]{1,0:T(8,128)(2,1)}, u32[]{:S(2)}) copy-start(bf16[128,128]{1,0:T(8,128)(2,1)} %param.33) | copy-start | bytes 98308
  7.2 75.6 %copy-start.1 = (bf16[128,1024]{1,0:T(8,128)(2,1)S(1)}, bf16[128,1024]{1,0:T(8,128)(2,1)}, u32[]{:S(2)}) copy-start(bf16[128,1024]{1,0:T(8,128)(2,1)} %param.32) | copy-start | bytes 786436
  7.2 75.7 %copy-start.7 = (f32[1024]{0:T(1024)S(1)}, f32[1024]{0:T(1024)}, u32[]{:S(2)}) copy-start(f32[1024]{0:T(1024)} %param.38) | copy-start | bytes 12292
  7.2 75.8 %copy-start.4 = (bf16[128,128]{1,0:T(8,128)(2,1)S(1)}, bf16[128,128]{1,0:T(8,128)(2,1)}, u32[]{:S(2)}) copy-start(bf16[128,128]{1,0:T(8,128)(2,1)} %param.30) | copy-start | bytes 98308
  7.2 76.0 %copy-start.5 = (bf16[128,128]{1,0:T(8,128)(2,1)S(1)}, bf16[128,128]{1,0:T(8,128)(2,1)}, u32[]{:S(2)}) copy-start(bf16[128,128]{1,0:T(8,128)(2,1)} %param.34) | copy-start | bytes 98308
  7.2 192.2 %all-gather.9.cloned.1.call-start = ((), (), s32[]{:S(2)}) async-start(), calls=%async_computation.2 | async-start | bytes 17039360 | tf_op jit(solution)/shard_map/all_gather | solution.py:22
  12.2 309.9 %reduce-scatter.4.cloned.1.call-start = ((), (), s32[]{:S(2)}) async-start(), calls=%async_computation.4 | async-start | bytes 294912
  199.5 73.2 %copy-start.8 = (f32[16]{0:T(128)S(1)}, f32[16]{0:T(128)}, u32[]{:S(2)}) copy-start(f32[16]{0:T(128)} %param.37) | copy-start | bytes 196
  288.8 35.5 %copy-start.2 = (bf16[128,512]{1,0:T(8,128)(2,1)S(1)}, bf16[128,512]{1,0:T(8,128)(2,1)}, u32[]{:S(2)}) copy-start(bf16[128,512]{1,0:T(8,128)(2,1)} %param.29) | copy-start | bytes 393220
  291.4 166.3 %all-gather.7.cloned.1.call-start = ((), (), s32[]{:S(2)}) async-start(), calls=%async_computation.1 | async-start | bytes 2129920 | tf_op jit(solution)/shard_map/all_gather | solution.py:102
  292.4 304.3 %all-gather.11.cloned.1.call-start = ((), (), s32[]{:S(2)}) async-start(), calls=%async_computation.3 | async-start | bytes 2129920 | tf_op jit(solution)/shard_map/all_gather | solution.py:103
Sparse Core Ops, SparseCore 0:
  12.3 187.0 all-gather.8
  291.6 30.4 reduce-scatter.3
  325.6 132.0 all-gather.6
  460.5 136.0 all-gather.10
where the time goes:
time: 895 us; the launch traced here: 883 us
  waiting for transfers between devices  411 us (46%)
  other arithmetic  135 us (15%)
  matrix products  134 us (15%)
  loops' own time  91.8 us (10%)
  blocking collectives  84.2 us (9%)
  between operations  14 us (2%)
  local copies, waits for them, and re-layouts  12.1 us (1%)
    all_gather x1, waiting for transfers between devices, attention(): piece_values = lax.all_gather(value_mat, 'ctx', axis=0, tiled=True)  134 us
    all_gather x1, waiting for transfers between devices, attention(): piece_keys = lax.all_gather(turned_k, 'ctx', axis=0, tiled=True)  133 us
    all_gather x1, waiting for transfers between devices, entering(): lax.all_gather(a.astype(kind), axis)  115 us
    another operation x1, loops' own time, attention(): result = lax.fori_loop(0, piece_rows // row_count, key_step, initial)  86 us
    all_gather x1, blocking collectives, entering(): lax.all_gather(a.astype(kind), axis)  70.4 us
    add x63, other arithmetic, chain_join(): jnp.exp(later[0])[:, None, None] * earlier[1] + later[1]  70 us
    dot_general x64, matrix products, attend_update(): jnp.einsum('cgts,scd->cgtd', weights.astype(jnp.bfloat16), value_block, p...  66.4 us
    dot_general x64, matrix products, attend_update(): jnp.einsum('cgtd,scd->cgts', query_group, key_block, preferred_element_ty...  61.9 us
  transfers between devices with their start and end apart: 4, of which 4 were waited for; matrix products, arithmetic and copies ran while one was open for 1% of the time, Pallas kernels for 0%

commit v1 on v0

--- a/solution.py
+++ b/solution.py
@@ -99,7 +99,8 @@
         jnp.zeros((kv_local, group_size, row_count), jnp.float32),
         jnp.zeros((kv_local, group_size, row_count, HEAD_DIM), jnp.float32),
     )
-    piece_keys = lax.all_gather(turned_k, "ctx", axis=0, tiled=True)
+    stack = jnp.stack([turned_k] * lax.axis_size("ctx"))
+    piece_keys = jnp.concatenate(lax.all_to_all(stack, "ctx", 0, 0), axis=0)
     piece_values = lax.all_gather(value_mat, "ctx", axis=0, tiled=True)
     piece_rows = piece_keys.shape[0]
     piece_pos = jnp.arange(piece_rows, dtype=jnp.int32)

time: 895 us -> 809 us (0.904)
  waiting for transfers between devices: 411 us -> 220 us
  blocking collectives: 84.2 us -> 192 us
  starting transfers between devices: 0.16 us -> 12.4 us
    all_gather x1 -> x0, waiting for transfers between devices: 133 us -> none  [attention(): piece_keys = lax.all_gather(turned_k, 'ctx', axis=0, tiled=True)]
    all_gather x1, blocking collectives: 70.4 us -> 178 us  [entering(): lax.all_gather(a.astype(kind), axis)]
    all_gather x1, waiting for transfers between devices: 115 us -> 52.3 us  [entering(): lax.all_gather(a.astype(kind), axis)]
    all_to_all x0 -> x1, starting transfers between devices: none -> 12.3 us  [attention(): piece_keys = jnp.concatenate(lax.all_to_all(stack, 'ctx', 0, 0), axis=0)]
    unnamed x5 -> x4, waiting for transfers between devices: 29.7 us -> 30.6 us
  transfers between devices with their start and end apart: 4 -> 4, of which waited for: 4 -> 3; matrix products, arithmetic and copies ran while one was open for 1% -> 11% of each run, Pallas kernels for 0% -> 0%
where the time goes in v1:
time: 809 us; the launch traced here: 797 us
  waiting for transfers between devices  220 us (27%)
  blocking collectives  192 us (24%)
  matrix products  134 us (17%)
  other arithmetic  130 us (16%)
  loops' own time  85.1 us (11%)
  between operations  14 us (2%)
  starting transfers between devices  12.4 us (2%)
  local copies, waits for them, and re-layouts  9.7 us (1%)
    all_gather x1, blocking collectives, entering(): lax.all_gather(a.astype(kind), axis)  178 us
    all_gather x1, waiting for transfers between devices, attention(): piece_values = lax.all_gather(value_mat, 'ctx', axis=0, tiled=True)  137 us
    another operation x1, loops' own time, attention(): result = lax.fori_loop(0, piece_rows // row_count, key_step, initial)  79.3 us
    add x63, other arithmetic, chain_join(): jnp.exp(later[0])[:, None, None] * earlier[1] + later[1]  70 us
    dot_general x64, matrix products, attend_update(): jnp.einsum('cgts,scd->cgtd', weights.astype(jnp.bfloat16), value_block, p...  66.4 us
    dot_general x64, matrix products, attend_update(): jnp.einsum('cgtd,scd->cgts', query_group, key_block, preferred_element_ty...  61.8 us
    all_gather x1, waiting for transfers between devices, entering(): lax.all_gather(a.astype(kind), axis)  52.3 us
    reduce_min x64, other arithmetic, key_step(): needed = jnp.min(block_pos) <= jnp.max(group_pos)  43.5 us
  transfers between devices with their start and end apart: 4, of which 3 were waited for; matrix products, arithmetic and copies ran while one was open for 11% of the time, Pallas kernels for 0%

profile of v1, /device:TPU:504, one launch (start us, length us, event | category | flops | bytes accessed | tf_op | source)
XLA Modules:
  0.0 796.9 jit_solution(4622335085679747239)
XLA Ops:
  15.2 12.3 %all-to-all-start = ((bf16[64,128,1,128]{3,1,2,0:T(8,128)(2,1)}), bf16[64,128,1,128]{3,1,2,0:T(8,128)(2,1)}, u32[]{:S(2)}, u32[]{:S(2)}) async-start(bf16[64,128,1,128]{3,1,2,0:T(8,128)(2,1)} %stack.2), calls=%async_computation | async-start | bytes 4194304 | tf_op jit(solution)/shard_map/all_to_all | solution.py:103
  27.6 177.6 %all-gather.2 = bf16[64,1,16]{2,1,0:T(2,128)(2,1)S(1)} all-gather(bf16[1,1,16]{2,1,0:T(2,128)(2,1)S(1)} %convert_bitcast_fusion), channel_id=1, replica_groups=mesh['ctx'=64,'exp'=8] {'ctx'}, dimensions={0}, use_global_device_ids=true | all-gather | bytes 2080 | tf_op jit(solution)/shard_map/all_gather | solution.py:22
  207.1 52.3 %all-gather.6.cloned.1.call-done = bf16[1024,64,128]{2,1,0:T(8,128)(2,1)} async-done(((bf16[16,64,128]{2,1,0:T(8,128)(2,1)}), bf16[1024,64,128]{2,1,0:T(8,128)(2,1)}) %all-gather.6.cloned.1.call-update) | async-done | bytes 16777232 | tf_op jit(solution)/shard_map/all_gather | solution.py:22
  259.5 73.1 %while.37 = (s32[]{:T(128)}, f32[16,64,128]{2,1,0:T(8,128)S(1)}, s32[]{:T(128)}, bf16[64,16]{1,0:T(8,128)(2,1)S(1)}, bf16[64,16,64,128]{3,2,1,0:T(8,128)(2,1)}, /*index=5*/s32[]{:T(128)}, s32[]{:T(128)}, s32[]{:T(128)}) while((s32[]{:T(128)}, f32[16,64,128]{2,1,0:T(8,128)S(1)}, s32[]{:T(128)}, bf16[64,16]{1,0:T(8,128)(2,1)S(1)}, ...), condition=%wide.region_2.3_spmd, body=%wide.region_1.2_spmd.sunk | while | flops 393237 | bytes 1311007 | solution.py:36
  332.6 2.3 multiply_reduce_fusion
  335.0 14.1 %psum.7 = f32[128]{0:T(128)S(1)} all-reduce(f32[128]{0:T(128)S(1)} %get-tuple-element.504), channel_id=1, replica_groups=mesh['ctx'=64,'exp'=8] {'exp'}, use_global_device_ids=true, to_apply=%region_4.5 | all-reduce | flops 128 | bytes 1024 | tf_op jit(solution)/shard_map/psum | solution.py:199
  351.8 30.6 %reduce-scatter.4.cloned.1.call-done = bf16[128,128]{1,0:T(8,128)(2,1)} async-done(((bf16[1024,128]{1,0:T(8,128)(2,1)}), bf16[128,128]{1,0:T(8,128)(2,1)}) %reduce-scatter.4.cloned.1.call-update) | async-done | bytes 32784
  385.9 137.2 %all-gather.8.cloned.1.call-done = bf16[8192,128]{1,0:T(8,128)(2,1)} async-done(((bf16[128,128]{1,0:T(8,128)(2,1)}), bf16[8192,128]{1,0:T(8,128)(2,1)}) %all-gather.8.cloned.1.call-update) | async-done | bytes 2097168 | tf_op jit(solution)/shard_map/all_gather | solution.py:104
  523.2 266.2 %while.38 = (s32[]{:T(128)}, f32[1,4,128]{2,1,0:T(4,128)S(1)}, f32[1,4,128]{2,1,0:T(4,128)S(1)}, f32[1,4,128,128]{3,2,1,0:T(8,128)S(1)}, s32[8192]{0:T(1024)S(1)...) while((s32[]{:T(128)}, f32[1,4,128]{2,1,0:T(4,128)S(1)}, ...), condition=%wide.region_13.14_spmd.clone, body=%wide.region_7.0_spmd.clone.sunk | while | flops 34293512 | bytes 1610581 | solution.py:135
  525.1 2.2 conditional.3
  529.3 2.2 conditional.3
  533.4 2.2 conditional.3
  537.6 2.2 conditional.3
  541.7 2.2 conditional.3
  545.9 2.2 conditional.3
  550.1 2.2 conditional.3
  554.2 2.2 conditional.3
  558.4 2.2 conditional.3
  562.5 2.2 conditional.3
  566.7 2.2 conditional.3
  570.9 2.2 conditional.3
  575.0 2.2 conditional.3
  579.2 2.2 conditional.3
  583.3 2.2 conditional.3
  587.5 2.2 conditional.3
  591.7 2.2 conditional.3
  595.8 2.2 conditional.3
  600.0 2.2 conditional.3
  604.1 2.2 conditional.3
  608.3 2.2 conditional.3
  612.5 2.2 conditional.3
  616.6 2.2 conditional.3
  620.8 2.2 conditional.3
  624.9 2.2 conditional.3
  629.1 2.2 conditional.3
  633.3 2.2 conditional.3
  637.4 2.2 conditional.3
  641.6 2.2 conditional.3
  645.7 2.2 conditional.3
  649.9 2.2 conditional.3
  654.1 2.2 conditional.3
  658.2 2.2 conditional.3
  662.4 2.2 conditional.3
  666.5 2.2 conditional.3
  670.7 2.2 conditional.3
  674.9 2.2 conditional.3
  679.0 2.2 conditional.3
  683.2 2.2 conditional.3
  (857 shorter events, 327.4 us)
Async XLA Ops:
  7.2 343.2 %copy-start = (bf16[1024,1024]{1,0:T(8,128)(2,1)S(1)}, bf16[1024,1024]{1,0:T(8,128)(2,1)}, u32[]{:S(2)}) copy-start(bf16[1024,1024]{1,0:T(8,128)(2,1)} %param.39) | copy-start | bytes 6291460
  7.2 252.2 %all-gather.6.cloned.1.call-start = ((), (), s32[]{:S(2)}) async-start(), calls=%async_computation.2 | async-start | bytes 17039360 | tf_op jit(solution)/shard_map/all_gather | solution.py:22
  15.2 190.1 %copy-start.1 = (bf16[128,1024]{1,0:T(8,128)(2,1)S(1)}, bf16[128,1024]{1,0:T(8,128)(2,1)}, u32[]{:S(2)}) copy-start(bf16[128,1024]{1,0:T(8,128)(2,1)} %param.32) | copy-start | bytes 786436
  15.2 190.3 %copy-start.6 = (f32[1024]{0:T(1024)S(1)}, f32[1024]{0:T(1024)}, u32[]{:S(2)}) copy-start(f32[1024]{0:T(1024)} %param.38) | copy-start | bytes 12292
  15.2 190.4 %copy-start.3 = (bf16[128,128]{1,0:T(8,128)(2,1)S(1)}, bf16[128,128]{1,0:T(8,128)(2,1)}, u32[]{:S(2)}) copy-start(bf16[128,128]{1,0:T(8,128)(2,1)} %param.33) | copy-start | bytes 98308
  15.2 190.4 %copy-start.4 = (bf16[128,128]{1,0:T(8,128)(2,1)S(1)}, bf16[128,128]{1,0:T(8,128)(2,1)}, u32[]{:S(2)}) copy-start(bf16[128,128]{1,0:T(8,128)(2,1)} %param.34) | copy-start | bytes 98308
  15.2 190.5 %copy-start.5 = (f32[128,16]{0,1:T(8,128)S(1)}, f32[128,16]{0,1:T(8,128)}, u32[]{:S(2)}) copy-start(f32[128,16]{0,1:T(8,128)} %param.35) | copy-start | bytes 24580
  15.2 370.7 %all-to-all-start = ((bf16[64,128,1,128]{3,1,2,0:T(8,128)(2,1)}), bf16[64,128,1,128]{3,1,2,0:T(8,128)(2,1)}, u32[]{:S(2)}, u32[]{:S(2)}) async-start(bf16[64,128,1,128]{3,1,2,0:T(8,128)(2,1)} %stack.2), calls=%async_computation | async-start | bytes 4194304 | tf_op jit(solution)/shard_map/all_to_all | solution.py:103
  27.5 354.8 %reduce-scatter.4.cloned.1.call-start = ((), (), s32[]{:S(2)}) async-start(), calls=%async_computation.4 | async-start | bytes 294912
  259.5 73.1 %copy-start.7 = (f32[16]{0:T(128)S(1)}, f32[16]{0:T(128)}, u32[]{:S(2)}) copy-start(f32[16]{0:T(128)} %param.37) | copy-start | bytes 196
  349.1 35.5 %copy-start.2 = (bf16[128,512]{1,0:T(8,128)(2,1)S(1)}, bf16[128,512]{1,0:T(8,128)(2,1)}, u32[]{:S(2)}) copy-start(bf16[128,512]{1,0:T(8,128)(2,1)} %param.29) | copy-start | bytes 393220
  351.7 171.4 %all-gather.8.cloned.1.call-start = ((), (), s32[]{:S(2)}) async-start(), calls=%async_computation.3 | async-start | bytes 2129920 | tf_op jit(solution)/shard_map/all_gather | solution.py:104
Sparse Core Ops, SparseCore 0:
  12.2 247.1 all-gather.5
  351.8 30.4 reduce-scatter.3
  385.9 137.2 all-gather.7
